TPU v7x, 32 devices: a whole 2x2x4 slice. The times are simulated.
32 devices in a mesh: seq: 4 (over y, core), vocab: 8 (over z, x).
Axes of the slice: x: 2, y: 2, z: 4, core: 2. Of those that a mesh axis runs over, the one named last changes fastest.
Arguments:
- hidden: bfloat16 [2, 512, 5120], P(None, 'seq'), may hold values from -128 to 128
- head_weight: bfloat16 [5120, 77824], P('seq', 'vocab'), may hold values from -1 to 1
- ref_logits: bfloat16 [2, 512, 77824], P(None, 'seq', 'vocab'), may hold values from -320 to 320
- token_ids: int32 [2, 512], P(None, 'seq'), may hold values from 0 to 77823
- end_pos: int32 [2], replicated, may hold values from 256 to 511
- loss_mask: int32 [2, 512], P(None, 'seq'), may hold values 0 or 1
- scores: float32 [2], replicated, may hold values from -8 to 8
Outputs:
- logit_grad: bfloat16 [2, 512, 77824], P(None, 'seq', 'vocab')
- hidden_grad: bfloat16 [2, 512, 5120], P(None, 'seq', 'vocab')
- advantages: float32 [2, 512], P(None, 'seq')
All inputs are finite; a program needn't handle non-finite values. No bound on the sum of `loss_mask` on one device may be relied on, other than what follows from the above.
Results may differ from a plain program's by a relative error of at most 0.0039.
The roundings to bfloat16 on the way count: a program that leaves them out, or rounds other values in their place, can miss the bound.
Values may be sent and summed in bfloat16 or wider, within the bound.
A program may use at most 128 MiB of HBM per device.

v0:
```python
import jax
import jax.numpy as jnp
from jax import lax
from jax.sharding import PartitionSpec as P


def from_behind(shard, axis, by):
    devices = lax.axis_size(axis)
    pairs = [(i, i + by) for i in range(devices) if 0 <= i + by < devices]
    return lax.ppermute(shard, axis, pairs)


def per_device(hidden, head_weight, ref_logits, token_ids, end_pos, loss_mask, scores):
    batch, segment, width = hidden.shape
    vocab_dev = head_weight.shape[1]
    seq_start = lax.axis_index("seq") * segment
    vocab_start = lax.axis_index("vocab") * vocab_dev
    split_hidden = lax.all_to_all(hidden, "seq", split_axis=2, concat_axis=1, tiled=True)
    logits = jnp.transpose(
        lax.psum_scatter(
            jnp.einsum(
                "bsd,dv->sbv", split_hidden, head_weight, preferred_element_type=jnp.float32
            ),
            "seq",
            scatter_dimension=0,
            tiled=True,
        ),
        (1, 0, 2),
    )
    refs = ref_logits.astype(jnp.float32)
    local_top = jnp.max(logits, axis=2)
    local_rtop = jnp.max(refs, axis=2)
    top_policy, top_ref = lax.pmax((local_top, local_rtop), "vocab")
    expo = jnp.exp(logits - top_policy[:, :, None])
    total, ref_total, weighted = lax.psum(
        (
            jnp.sum(expo, axis=2),
            jnp.sum(jnp.exp(refs - top_ref[:, :, None]), axis=2),
            jnp.sum(expo * (logits - refs), axis=2),
        ),
        "vocab",
    )
    lse_policy = top_policy + jnp.log(total)
    lse_ref = top_ref + jnp.log(ref_total)
    kl_value = weighted / total - lse_policy + lse_ref
    position = seq_start + lax.broadcasted_iota(jnp.int32, (1, segment), 1)
    live = ((loss_mask == 1) & (position <= end_pos[:, None])).astype(jnp.float32)
    at_end = (position == end_pos[:, None]).astype(jnp.float32)
    reward = -0.01 * kl_value * live + scores[:, None] * at_end
    upper = (
        lax.broadcasted_iota(jnp.int32, (segment, segment), 0)
        >= lax.broadcasted_iota(jnp.int32, (segment, segment), 1)
    ).astype(jnp.float32)
    local_returns = jnp.dot(reward, upper, precision=lax.Precision.HIGHEST)
    totals = jnp.sum(reward, axis=1)
    carried = jnp.zeros_like(totals)
    for _ in range(lax.axis_size("seq") - 1):
        carried = from_behind(totals + carried, "seq", -1)
    returns = local_returns + carried[:, None]
    count, first_moment, second_moment = lax.psum(
        (jnp.sum(live), jnp.sum(live * returns), jnp.sum(live * returns * returns)), "seq"
    )
    count = jnp.maximum(count, 1.0)
    mean = first_moment / count
    var = second_moment / count - mean * mean
    advantages = (returns - mean) / jnp.sqrt(var + 1e-05)
    factor = live * advantages / count
    prob = jnp.exp(logits - lse_policy[:, :, None])
    column = vocab_start + lax.broadcasted_iota(jnp.int32, (1, 1, vocab_dev), 2)
    onehot = (column == token_ids[:, :, None]).astype(jnp.float32)
    logit_grad = (factor[:, :, None] * (prob - onehot)).astype(jnp.bfloat16)
    all_grads = lax.all_gather(logit_grad, "seq", axis=1, tiled=True)
    slice_grad = jnp.einsum(
        "bsv,dv->bsd", all_grads, head_weight, preferred_element_type=jnp.float32
    )
    partial_grad = lax.all_to_all(slice_grad, "seq", split_axis=1, concat_axis=2, tiled=True)
    hidden_grad = lax.psum_scatter(partial_grad, "vocab", scatter_dimension=2, tiled=True).astype(
        jnp.bfloat16
    )
    return (logit_grad, hidden_grad, advantages)


def solution(mesh):
    in_specs = (
        P(None, "seq", None),
        P("seq", "vocab"),
        P(None, "seq", "vocab"),
        P(None, "seq"),
        P(),
        P(None, "seq"),
        P(),
    )
    out_specs = (P(None, "seq", "vocab"), P(None, "seq", "vocab"), P(None, "seq"))
    return jax.shard_map(
        per_device, mesh=mesh, in_specs=in_specs, out_specs=out_specs, check_vma=False
    )
```

profile of v0, /device:TPU:0, one launch (start us, length us, event | category | flops | bytes accessed | tf_op | source)
XLA Modules:
  0.0 799.1 jit_solution(6188763925158385231)
XLA Ops:
  7.2 0.0 reduce-scatter.3.cloned.1.call-start
  7.2 7.4 copy.16
  14.6 35.6 %all_to_all.36 = bf16[2,128,5120]{1,0,2:T(2,128)(2,1)S(1)} all-to-all(bf16[2,128,5120]{1,0,2:T(2,128)(2,1)} %copy.16), channel_id=1, replica_groups=mesh['seq'=4,'vocab'=8] {'seq'}, dimensions={2} | all-to-all | bytes 5242880 | tf_op jit(solution)/shard_map/all_to_all | solution.py:18
  50.2 4.6 copy.17
  54.9 34.2 %fusion.4 = f32[512,2,9728]{0,2,1:T(8,128)} fusion(bf16[2,512,1280]{2,1,0:T(8,128)(2,1)} %bitcast.41, bf16[1280,9728]{1,0:T(8,128)(2,1)} %param.8), kind=kOutput, calls=%fused_computation.4 | convolution fusion | flops 25501368320 | bytes 67371008 | tf_op jit(solution)/shard_map/bsd,dv->sbv/dot_general | solution.py:21
  89.1 0.0 reduce-scatter.3.cloned.1.call-update
  89.1 0.0 all-gather.2.cloned.1.call-start
  89.1 8.0 copy.19
  97.1 4.5 reduce_max.24
  101.6 258.7 %reduce-scatter.3.cloned.1.call-done = f32[128,2,9728]{0,2,1:T(8,128)} async-done(((f32[512,2,9728]{0,2,1:T(8,128)}), f32[128,2,9728]{0,2,1:T(8,128)}) %reduce-scatter.3.cloned.1.call-update) | async-done | bytes 9961488 | tf_op jit(solution)/shard_map/reduce_scatter | solution.py:20
  360.3 4.6 bitcast_reduce_fusion
  364.9 0.0 copy-start
  364.9 0.0 copy-start.2
  364.9 0.0 copy-start.3
  364.9 0.0 copy-start.1
  364.9 21.3 %all-reduce.1 = (f32[2,128]{1,0:T(2,128)S(1)}, f32[2,128]{1,0:T(2,128)S(1)}) all-reduce(f32[2,128]{1,0:T(2,128)S(1)} %bitcast_reduce_fusion, bf16[2,128]{1,0:T(2,128)(2,1)S(1)} %reduce_max.24), channel_id=1, replica_groups=mesh['seq'=4,'vocab'=8] {'vocab'}, use_global_device_ids=true, to_apply=%region_2.0 | all-reduce | flops 512 | bytes 3584 | tf_op jit(solution)/shard_map/pmax | solution.py:33
  386.3 7.5 fusion.8
  393.8 17.1 %all-reduce = (f32[2,128]{1,0:T(2,128)S(1)}, f32[2,128]{1,0:T(2,128)S(1)}, f32[2,128]{1,0:T(2,128)S(1)}) all-reduce(f32[2,128]{1,0:T(2,128)S(1)} %get-tuple-element.10, f32[2,128]{1,0:T(2,128)S(1)} %get-tuple-element.11, f32[2,128]{1,0:T(2,128)S(1)} %get-tuple-element.9), channel_id=1, replica_groups=mesh['seq'=4,'vocab'=8] {'vocab'}, use_global_device_ids=true, to_apply=%region_6.0 | all-reduce | flops 768 | bytes 6144 | tf_op jit(solution)/shard_map/psum | solution.py:35
  411.0 0.0 copy-done
  411.0 0.0 copy-done.2
  411.0 0.0 copy-done.3
  411.0 0.2 fusion.20
  411.2 1.3 collective-permute-start
  412.5 1.8 collective-permute-done
  414.2 1.3 collective-permute-start.1
  415.5 2.0 collective-permute-done.1
  417.6 1.3 collective-permute-start.2
  418.8 3.6 collective-permute-done.2
  422.4 0.8 select_reduce_fusion
  423.2 8.8 %all-reduce.2 = (f32[]{:T(128)}, f32[]{:T(128)}, f32[]{:T(128)}) all-reduce(f32[]{:T(128)} %get-tuple-element.13, f32[]{:T(128)} %get-tuple-element.14, f32[]{:T(128)} %get-tuple-element.12), channel_id=1, replica_groups=mesh['seq'=4,'vocab'=8] {'seq'}, use_global_device_ids=true, to_apply=%region_17.0 | all-reduce | flops 3 | bytes 24 | tf_op jit(solution)/shard_map/psum | solution.py:60
  434.0 0.6 select_divide_fusion
  434.6 0.0 copy-done.1
  434.6 9.3 %fusion.16 = bf16[2,128,9728]{1,2,0:T(8,128)(2,1)} fusion(f32[128,2,9728]{0,2,1:T(8,128)} %reduce-scatter.3.cloned.1.call-done, s32[2,128]{1,0:T(2,128)S(1)} %copy-done.1, f32[2,128]{1,0:T(2,128)S(1)} %get-tuple-element.28, f32[2,128]{1,0:T(2,128)S(1)} %get-tuple-element.23, s32[9728]{0:T(1024)S(1)} %iota_add_fusion), kind=kLoop, calls=%fused_computation.19 | loop fusion | flops 14942208 | bytes 14984192 | tf_op jit(solution)/shard_map/convert_element_type | solution.py:71
  443.9 0.0 all-gather.2.cloned.1.call-update
  444.0 0.0 reduce-scatter.5.cloned.1.call-start
  444.0 127.4 %all-gather.2.cloned.1.call-done = bf16[2,512,9728]{1,2,0:T(8,128)(2,1)} async-done(((bf16[2,128,9728]{1,2,0:T(8,128)(2,1)}), bf16[2,512,9728]{1,2,0:T(8,128)(2,1)}) %all-gather.2.cloned.1.call-update) | async-done | bytes 19922960 | tf_op jit(solution)/shard_map/all_gather | solution.py:72
  571.4 34.7 %fusion = f32[2,512,1280]{2,1,0:T(8,128)} fusion(bf16[2,512,9728]{1,2,0:T(8,128)(2,1)} %all-gather.2.cloned.1.call-done, bf16[1280,9728]{1,0:T(8,128)(2,1)} %param.8), kind=kOutput, calls=%fused_computation | convolution fusion | flops 25501368320 | bytes 50069504 | tf_op jit(solution)/shard_map/bsv,dv->bsd/dot_general | solution.py:73
  606.1 6.5 copy.21
  612.7 62.0 %all_to_all.37 = f32[2,512,1280]{2,0,1:T(2,128)S(1)} all-to-all(f32[2,512,1280]{2,0,1:T(2,128)S(1)} %copy.21), channel_id=1, replica_groups=mesh['seq'=4,'vocab'=8] {'seq'}, dimensions={1} | all-to-all | bytes 10485760 | tf_op jit(solution)/shard_map/all_to_all | solution.py:76
  674.7 5.7 copy.22
  680.4 7.2 all_to_all.33
  687.6 0.0 reduce-scatter.5.cloned.1.call-update
  687.6 7.9 copy.23
  695.5 95.3 %reduce-scatter.5.cloned.1.call-done = f32[2,128,640]{2,1,0:T(8,128)} async-done(((f32[2,128,5120]{2,1,0:T(8,128)}), f32[2,128,640]{2,1,0:T(8,128)}) %reduce-scatter.5.cloned.1.call-update) | async-done | bytes 655376 | tf_op jit(solution)/shard_map/reduce_scatter | solution.py:77
  790.8 1.8 convert_element_type.21
  (4 shorter events, 0.0 us)
Async XLA Ops:
  7.2 353.2 %reduce-scatter.3.cloned.1.call-start = ((), (), s32[]{:S(2)}) async-start(), calls=%async_computation.4 | async-start | bytes 49807360 | tf_op jit(solution)/shard_map/reduce_scatter | solution.py:20
  89.1 482.3 %all-gather.2.cloned.1.call-start = ((), (), s32[]{:S(2)}) async-start(), calls=%async_computation.5 | async-start | bytes 24903680 | tf_op jit(solution)/shard_map/all_gather | solution.py:72
  364.9 46.1 %copy-start = (s32[2,128]{1,0:T(2,128)S(1)}, s32[2,128]{1,0:T(2,128)}, u32[]{:S(2)}) copy-start(s32[2,128]{1,0:T(2,128)} %param.12) | copy-start | bytes 3076
  364.9 46.1 %copy-start.2 = (f32[2]{0:T(128)S(1)}, f32[2]{0:T(128)}, u32[]{:S(2)}) copy-start(f32[2]{0:T(128)} %param.13) | copy-start | bytes 28
  364.9 46.1 %copy-start.3 = (s32[2]{0:T(128)S(1)}, s32[2]{0:T(128)}, u32[]{:S(2)}) copy-start(s32[2]{0:T(128)} %param.11) | copy-start | bytes 28
  364.9 69.7 %copy-start.1 = (s32[2,128]{1,0:T(2,128)S(1)}, s32[2,128]{1,0:T(2,128)}, u32[]{:S(2)}) copy-start(s32[2,128]{1,0:T(2,128)} %param.10) | copy-start | bytes 3076
  411.2 3.0 collective-permute-start
  414.2 3.3 collective-permute-start.1
  417.6 4.9 collective-permute-start.2
  444.0 346.8 %reduce-scatter.5.cloned.1.call-start = ((), (), s32[]{:S(2)}) async-start(), calls=%async_computation.6 | async-start | bytes 5898240 | tf_op jit(solution)/shard_map/reduce_scatter | solution.py:77
Sparse Core Ops, SparseCore 0:
  89.2 271.0 reduce-scatter.2
  444.1 127.2 all-gather.1
  687.7 102.9 reduce-scatter.4
where the time goes:
time: 800 us; the launch traced here: 799 us
  waiting for transfers between devices  489 us (61%)
  blocking collectives  145 us (18%)
  matrix products  69.7 us (9%)
  local copies, waits for them, and re-layouts  47.4 us (6%)
  other arithmetic  28.6 us (4%)
  between operations  15.8 us (2%)
    reduce_scatter x1, waiting for transfers between devices, per_device(): lax.psum_scatter(jnp.einsum('bsd,dv->sbv', split_hidden, head_weight, pre...  259 us
    all_gather x1, waiting for transfers between devices, per_device(): all_grads = lax.all_gather(logit_grad, 'seq', axis=1, tiled=True)  127 us
    reduce_scatter x1, waiting for transfers between devices, per_device(): lax.psum_scatter(partial_grad, 'vocab', scatter_dimension=2, tiled=True)  95.3 us
    all_to_all x1, blocking collectives, per_device(): lax.all_to_all(slice_grad, 'seq', split_axis=1, concat_axis=2, tiled=True)  62 us
    all_to_all x1, blocking collectives, per_device(): lax.all_to_all(hidden, 'seq', split_axis=2, concat_axis=1, tiled=True)  35.6 us
    dot_general x1, matrix products, per_device(): jnp.einsum('bsv,dv->bsd', all_grads, head_weight, preferred_element_type=...  34.7 us
    dot_general x1, matrix products, per_device(): jnp.einsum('bsd,dv->sbv', split_hidden, head_weight, preferred_element_ty...  34.2 us
    unnamed x11, local copies, waits for them, and re-layouts  23.3 us
  transfers between devices with their start and end apart: 6, of which 6 were waited for; matrix products, arithmetic and copies ran while one was open for 3% of the time, Pallas kernels for 0%

commit v1 on v0

--- a/solution.py
+++ b/solution.py
@@ -73,7 +73,10 @@
     slice_grad = jnp.einsum(
         "bsv,dv->bsd", all_grads, head_weight, preferred_element_type=jnp.float32
     )
-    partial_grad = lax.all_to_all(slice_grad, "seq", split_axis=1, concat_axis=2, tiled=True)
+    peers = lax.axis_size("seq")
+    parts = jnp.stack(jnp.split(slice_grad, peers, axis=1), axis=0)
+    parts = lax.all_to_all(parts, "seq", split_axis=0, concat_axis=0)
+    partial_grad = jnp.concatenate(parts, axis=2)
     hidden_grad = lax.psum_scatter(partial_grad, "vocab", scatter_dimension=2, tiled=True).astype(
         jnp.bfloat16
     )

time: 800 us -> 791 us (0.989)
  local copies, waits for them, and re-layouts: 47.4 us -> 37.7 us
    all_to_all x2 -> x0, local copies, waits for them, and re-layouts: 12.9 us -> none  [per_device(): lax.all_to_all(slice_grad, 'seq', split_axis=1, concat_axis=2, tiled=True)]
    unnamed x11 -> x12, local copies, waits for them, and re-layouts: 23.3 us -> 24.2 us
where the time goes in v1:
time: 791 us; the launch traced here: 790 us
  waiting for transfers between devices  489 us (62%)
  blocking collectives  146 us (18%)
  matrix products  69.7 us (9%)
  local copies, waits for them, and re-layouts  37.7 us (5%)
  other arithmetic  28.3 us (4%)
  between operations  15.8 us (2%)
    reduce_scatter x1, waiting for transfers between devices, per_device(): lax.psum_scatter(jnp.einsum('bsd,dv->sbv', split_hidden, head_weight, pre...  259 us
    all_gather x1, waiting for transfers between devices, per_device(): all_grads = lax.all_gather(logit_grad, 'seq', axis=1, tiled=True)  127 us
    reduce_scatter x1, waiting for transfers between devices, per_device(): lax.psum_scatter(partial_grad, 'vocab', scatter_dimension=2, tiled=True)  95.2 us
    all_to_all x1, blocking collectives, per_device(): parts = lax.all_to_all(parts, 'seq', split_axis=0, concat_axis=0)  62.9 us
    all_to_all x1, blocking collectives, per_device(): lax.all_to_all(hidden, 'seq', split_axis=2, concat_axis=1, tiled=True)  35.6 us
    dot_general x1, matrix products, per_device(): jnp.einsum('bsv,dv->bsd', all_grads, head_weight, preferred_element_type=...  34.7 us
    dot_general x1, matrix products, per_device(): jnp.einsum('bsd,dv->sbv', split_hidden, head_weight, preferred_element_ty...  34.2 us
    unnamed x12, local copies, waits for them, and re-layouts  24.2 us
  transfers between devices with their start and end apart: 6, of which 6 were waited for; matrix products, arithmetic and copies ran while one was open for 3% of the time, Pallas kernels for 0%

profile of v1, /device:TPU:0, one launch (start us, length us, event | category | flops | bytes accessed | tf_op | source)
XLA Modules:
  0.0 790.0 jit_solution(3842077865711002288)
XLA Ops:
  7.2 0.0 reduce-scatter.3.cloned.1.call-start
  7.2 7.4 copy.22
  14.6 35.6 %all_to_all.23 = bf16[2,128,5120]{1,0,2:T(2,128)(2,1)S(1)} all-to-all(bf16[2,128,5120]{1,0,2:T(2,128)(2,1)} %copy.22), channel_id=1, replica_groups=mesh['seq'=4,'vocab'=8] {'seq'}, dimensions={2} | all-to-all | bytes 5242880 | tf_op jit(solution)/shard_map/all_to_all | solution.py:18
  50.2 4.6 copy.23
  54.9 34.2 %fusion.4 = f32[512,2,9728]{0,2,1:T(8,128)} fusion(bf16[2,512,1280]{2,1,0:T(8,128)(2,1)} %bitcast.49, bf16[1280,9728]{1,0:T(8,128)(2,1)} %param.8), kind=kOutput, calls=%fused_computation.4 | convolution fusion | flops 25501368320 | bytes 67371008 | tf_op jit(solution)/shard_map/bsd,dv->sbv/dot_general | solution.py:21
  89.1 0.0 reduce-scatter.3.cloned.1.call-update
  89.1 0.0 all-gather.2.cloned.1.call-start
  89.1 8.0 %copy.25 = bf16[2,128,9728]{1,2,0:T(8,128)(2,1)} copy(bf16[2,128,9728]{2,1,0:T(8,128)(2,1)} %param.9) | data formatting | bytes 9961472 | tf_op args[2]
  97.1 4.5 reduce_max.24
  101.6 258.7 %reduce-scatter.3.cloned.1.call-done = f32[128,2,9728]{0,2,1:T(8,128)} async-done(((f32[512,2,9728]{0,2,1:T(8,128)}), f32[128,2,9728]{0,2,1:T(8,128)}) %reduce-scatter.3.cloned.1.call-update) | async-done | bytes 9961488 | tf_op jit(solution)/shard_map/reduce_scatter | solution.py:20
  360.3 4.6 bitcast_reduce_fusion
  364.9 21.3 %all-reduce.1 = (f32[2,128]{1,0:T(2,128)S(1)}, f32[2,128]{1,0:T(2,128)S(1)}) all-reduce(f32[2,128]{1,0:T(2,128)S(1)} %bitcast_reduce_fusion, bf16[2,128]{1,0:T(2,128)(2,1)S(1)} %reduce_max.24), channel_id=1, replica_groups=mesh['seq'=4,'vocab'=8] {'vocab'}, use_global_device_ids=true, to_apply=%region_2.0 | all-reduce | flops 512 | bytes 3584 | tf_op jit(solution)/shard_map/pmax | solution.py:33
  386.2 0.0 copy-start
  386.2 0.0 copy-start.2
  386.3 0.0 copy-start.3
  386.3 0.0 copy-start.1
  386.3 7.6 fusion.8
  393.8 17.1 %all-reduce = (f32[2,128]{1,0:T(2,128)S(1)}, f32[2,128]{1,0:T(2,128)S(1)}, f32[2,128]{1,0:T(2,128)S(1)}) all-reduce(f32[2,128]{1,0:T(2,128)S(1)} %get-tuple-element.13, f32[2,128]{1,0:T(2,128)S(1)} %get-tuple-element.14, f32[2,128]{1,0:T(2,128)S(1)} %get-tuple-element.12), channel_id=1, replica_groups=mesh['seq'=4,'vocab'=8] {'vocab'}, use_global_device_ids=true, to_apply=%region_6.0 | all-reduce | flops 768 | bytes 6144 | tf_op jit(solution)/shard_map/psum | solution.py:35
  411.0 0.0 copy-done
  411.0 0.0 copy-done.2
  411.0 0.0 copy-done.3
  411.0 0.2 fusion.20
  411.2 1.3 collective-permute-start
  412.5 1.8 collective-permute-done
  414.2 1.3 collective-permute-start.1
  415.5 2.0 collective-permute-done.1
  417.6 1.3 collective-permute-start.2
  418.9 3.6 collective-permute-done.2
  422.4 0.8 select_reduce_fusion
  423.2 8.8 %all-reduce.2 = (f32[]{:T(128)}, f32[]{:T(128)}, f32[]{:T(128)}) all-reduce(f32[]{:T(128)} %get-tuple-element.16, f32[]{:T(128)} %get-tuple-element.17, f32[]{:T(128)} %get-tuple-element.15), channel_id=1, replica_groups=mesh['seq'=4,'vocab'=8] {'seq'}, use_global_device_ids=true, to_apply=%region_17.0 | all-reduce | flops 3 | bytes 24 | tf_op jit(solution)/shard_map/psum | solution.py:60
  434.0 0.6 select_divide_fusion
  434.6 0.0 copy-done.1
  434.6 9.3 %fusion.16 = bf16[2,128,9728]{1,2,0:T(8,128)(2,1)} fusion(f32[128,2,9728]{0,2,1:T(8,128)} %reduce-scatter.3.cloned.1.call-done, s32[2,128]{1,0:T(2,128)S(1)} %copy-done.1, f32[2,128]{1,0:T(2,128)S(1)} %get-tuple-element.31, f32[2,128]{1,0:T(2,128)S(1)} %get-tuple-element.26, s32[9728]{0:T(1024)S(1)} %iota_add_fusion), kind=kLoop, calls=%fused_computation.19 | loop fusion | flops 14942208 | bytes 14984192 | tf_op jit(solution)/shard_map/convert_element_type | solution.py:71
  444.0 0.0 all-gather.2.cloned.1.call-update
  444.0 0.0 reduce-scatter.5.cloned.1.call-start
  444.0 127.4 %all-gather.2.cloned.1.call-done = bf16[2,512,9728]{1,2,0:T(8,128)(2,1)} async-done(((bf16[2,128,9728]{1,2,0:T(8,128)(2,1)}), bf16[2,512,9728]{1,2,0:T(8,128)(2,1)}) %all-gather.2.cloned.1.call-update) | async-done | bytes 19922960 | tf_op jit(solution)/shard_map/all_gather | solution.py:72
  571.4 34.7 %fusion = f32[2,512,1280]{2,1,0:T(8,128)} fusion(bf16[2,512,9728]{1,2,0:T(8,128)(2,1)} %all-gather.2.cloned.1.call-done, bf16[1280,9728]{1,0:T(8,128)(2,1)} %param.8), kind=kOutput, calls=%fused_computation | convolution fusion | flops 25501368320 | bytes 50069504 | tf_op jit(solution)/shard_map/bsv,dv->bsd/dot_general | solution.py:73
  606.2 2.9 slice_bitcast_fusion.3
  609.1 0.4 pad_maximum_fusion
  609.5 62.9 %all_to_all.24 = f32[4,2,128,1280]{3,2,1,0:T(8,128)} all-to-all(f32[4,2,128,1280]{3,2,1,0:T(8,128)S(1)} %pad_maximum_fusion), channel_id=1, replica_groups=mesh['seq'=4,'vocab'=8] {'seq'}, dimensions={0} | all-to-all | bytes 10485760 | tf_op jit(solution)/shard_map/all_to_all | solution.py:78
  672.4 5.9 copy.27
  678.3 0.0 reduce-scatter.5.cloned.1.call-update
  678.3 7.9 %copy.28 = bf16[2,128,9728]{2,1,0:T(8,128)(2,1)} copy(bf16[2,128,9728]{1,2,0:T(8,128)(2,1)} %fusion.16) | data formatting | bytes 9961472
  686.2 95.2 %reduce-scatter.5.cloned.1.call-done = f32[2,128,640]{1,2,0:T(8,128)} async-done(((f32[2,128,5120]{1,2,0:T(8,128)}), f32[2,128,640]{1,2,0:T(8,128)}) %reduce-scatter.5.cloned.1.call-update) | async-done | bytes 655376 | tf_op jit(solution)/shard_map/reduce_scatter | solution.py:80
  781.5 1.1 convert_element_type.21
  782.6 0.9 copy.29
  (4 shorter events, 0.0 us)
Async XLA Ops:
  7.2 353.2 %reduce-scatter.3.cloned.1.call-start = ((), (), s32[]{:S(2)}) async-start(), calls=%async_computation.4 | async-start | bytes 49807360 | tf_op jit(solution)/shard_map/reduce_scatter | solution.py:20
  89.1 482.3 %all-gather.2.cloned.1.call-start = ((), (), s32[]{:S(2)}) async-start(), calls=%async_computation.5 | async-start | bytes 24903680 | tf_op jit(solution)/shard_map/all_gather | solution.py:72
  386.2 24.7 %copy-start = (s32[2,128]{1,0:T(2,128)S(1)}, s32[2,128]{1,0:T(2,128)}, u32[]{:S(2)}) copy-start(s32[2,128]{1,0:T(2,128)} %param.12) | copy-start | bytes 3076
  386.2 24.7 %copy-start.2 = (f32[2]{0:T(128)S(1)}, f32[2]{0:T(128)}, u32[]{:S(2)}) copy-start(f32[2]{0:T(128)} %param.13) | copy-start | bytes 28
  386.3 24.7 %copy-start.3 = (s32[2]{0:T(128)S(1)}, s32[2]{0:T(128)}, u32[]{:S(2)}) copy-start(s32[2]{0:T(128)} %param.11) | copy-start | bytes 28
  386.3 48.4 %copy-start.1 = (s32[2,128]{1,0:T(2,128)S(1)}, s32[2,128]{1,0:T(2,128)}, u32[]{:S(2)}) copy-start(s32[2,128]{1,0:T(2,128)} %param.10) | copy-start | bytes 3076
  411.2 3.0 collective-permute-start
  414.2 3.3 collective-permute-start.1
  417.6 4.9 collective-permute-start.2
  444.0 337.5 %reduce-scatter.5.cloned.1.call-start = ((), (), s32[]{:S(2)}) async-start(), calls=%async_computation.6 | async-start | bytes 5898240 | tf_op jit(solution)/shard_map/reduce_scatter | solution.py:80
Sparse Core Ops, SparseCore 0:
  89.2 271.0 reduce-scatter.2
  444.1 127.2 all-gather.1
  678.4 102.9 reduce-scatter.4
